TPU v7x, 128 devices: a whole 4x4x4 slice. The times are simulated.
128 devices in a mesh: expert: 4 (over z), seq: 4 (over y), tensor: 8 (over x, core).
Axes of the slice: x: 4, y: 4, z: 4, core: 2. Of those that a mesh axis runs over, the one named last changes fastest.
Arguments:
- tokens: bfloat16 [3072, 7168], P(('expert', 'seq')), may hold values from -6 to 6
- grad_out: bfloat16 [3072, 7168], P(('expert', 'seq')), may hold values from -6 to 6
- expert_ids: int32 [3072, 2], P(('expert', 'seq')), may hold values from 0 to 3, all different within a row; in each aligned block of 192 rows (0 to 191, 192 to 383, ...) at most 128 rows name the same one
- route_weights: bfloat16 [3072, 2], P(('expert', 'seq')), may hold values from 0.099609375 to 1
- gate_weight: bfloat16 [4, 7168, 2048], P('expert', 'seq', 'tensor'), may hold values from -0.0625 to 0.0625
- up_weight: bfloat16 [4, 7168, 2048], P('expert', 'seq', 'tensor'), may hold values from -0.0625 to 0.0625
- down_weight: bfloat16 [4, 7168, 2048], P('expert', 'seq', 'tensor'), may hold values from -0.125 to 0.125
Outputs:
- grad_tokens: bfloat16 [3072, 7168], P(('expert', 'seq'), 'tensor')
- grad_route: float32 [3072, 2], P(('expert', 'seq'))
- grad_gate: float32 [4, 7168, 2048], P('expert', 'seq', 'tensor')
- grad_up: float32 [4, 7168, 2048], P('expert', 'seq', 'tensor')
- grad_down: float32 [4, 7168, 2048], P('expert', 'seq', 'tensor')
Inputs may be any that keep to these rules, and one draw needn't show every extreme that they name: `expert_ids`: the two ids of a row differ. Within each aligned block of 192 rows (the tokens of one group of the expert and seq axes) no expert is named by more than 128 rows, and in some block an expert is named by exactly 128 rows.
All inputs are finite; a program needn't handle non-finite values.
Results may differ from a plain program's by a relative error of at most 0.019.
Values may be sent and summed in bfloat16 or wider, within the bound.
A program may use at most 192 MiB of HBM per device.

v0:
```python
import functools

import jax
import jax.numpy as jnp
from jax import lax
from jax.experimental import pallas as pl
from jax.experimental.pallas import tpu as pltpu
from jax.sharding import PartitionSpec as P

MESH = pl.DeviceIdType.MESH


def exchange_kernel(
    n_seq, n_tx, peers, tok_send, grad_send, tok_out, grad_out, send_sem, recv_sem, local_sem
):
    sends = (tok_send, grad_send)
    outs = (tok_out, grad_out)
    e = lax.axis_index("expert")
    s = lax.axis_index("seq")
    x = lax.axis_index("tx")
    c = lax.axis_index("core")
    me = e * n_seq + s
    other = 1 - c
    x_left = lax.rem(x + n_tx - 1, n_tx)
    x_right = lax.rem(x + 1, n_tx)
    x_far = lax.rem(x + 2, n_tx)
    own = x * 2 + c
    from_left = x_left * 2 + c
    from_right = x_right * 2 + c
    from_far = x_far * 2 + c
    left = (e, s, x_left, c)
    right = (e, s, x_right, c)
    partner = (e, s, x, other)

    def peer(k):
        q = lax.rem(me + k, peers)
        return q, (q // n_seq, q % n_seq, x, c)

    barrier = pltpu.get_barrier_semaphore()
    for k in range(1, peers):
        pl.semaphore_signal(barrier, inc=1, device_id=peer(k)[1], device_id_type=MESH)
    for where in (left, right, partner):
        pl.semaphore_signal(barrier, inc=1, device_id=where, device_id_type=MESH)
    pl.semaphore_wait(barrier, peers + 2)

    def remote(kind, src, dst, slot, recv, where):
        return pltpu.make_async_remote_copy(
            src_ref=src,
            dst_ref=dst,
            send_sem=send_sem.at[kind, slot],
            recv_sem=recv_sem.at[kind, recv],
            device_id=where,
            device_id_type=MESH,
        )

    locals_ = [
        pltpu.make_async_copy(sends[kind].at[me], outs[kind].at[own, me], local_sem.at[kind])
        for kind in range(2)
    ]
    for copy in locals_:
        copy.start()
    for k in range(1, peers):
        q, where = peer(k)
        for kind in range(2):
            remote(
                kind, sends[kind].at[q], outs[kind].at[own, me], q, own * peers + me, where
            ).start()

    def arrived(chunk, p):
        for kind in range(2):
            block = outs[kind].at[chunk, p]
            remote(kind, block, block, 0, chunk * peers + p, partner).wait_recv()

    def forward(chunk, p, slot, where):
        for kind in range(2):
            block = outs[kind].at[chunk, p]
            remote(kind, block, block, slot, chunk * peers + p, where).start()

    for copy in locals_:
        copy.wait()
    for k in range(peers):
        p = peer(k)[0]
        if k > 0:
            arrived(own, p)
        forward(own, p, peers + p, right)
        forward(own, p, 2 * peers + p, left)
        forward(own, p, 3 * peers + p, partner)

    def relay(chunk, onward, onward_parity, base):
        def body(i, carry):
            for parity in (0, 1):
                p = 2 * i + parity
                arrived(chunk, p)
                if onward is not None and parity == onward_parity:
                    forward(chunk, p, base + peers + p, onward)
                forward(chunk, p, base + p, partner)
            return carry

        lax.fori_loop(0, peers // 2, body, 0)

    relay(from_left, right, 0, 4 * peers)
    relay(from_right, left, 1, 6 * peers)
    relay(from_far, None, 0, 8 * peers)

    def partner_chunks(p, carry):
        for column in range(n_tx):
            arrived(column * 2 + other, p)
        return carry

    lax.fori_loop(0, peers, partner_chunks, 0)

    def drain(slot, carry):
        for kind in range(2):
            block = outs[kind].at[own, 0]
            remote(kind, block, block, slot, 0, partner).wait_send()
        return carry

    def drain_pairs(first, parity):
        def body(i, carry):
            return drain(first + 2 * i + parity, carry)

        lax.fori_loop(0, peers // 2, body, 0)

    for k in range(1, peers):
        drain(peer(k)[0], 0)
    lax.fori_loop(peers, 5 * peers, drain, 0)
    drain_pairs(5 * peers, 0)
    lax.fori_loop(6 * peers, 7 * peers, drain, 0)
    drain_pairs(7 * peers, 1)
    lax.fori_loop(8 * peers, 9 * peers, drain, 0)


def exchange_rows(tok_send, grad_send, n_seq, n_tx):
    peers = tok_send.shape[0]
    chunks = 2 * n_tx
    shape = jax.ShapeDtypeStruct((chunks,) + tok_send.shape, tok_send.dtype)
    return pl.pallas_call(
        functools.partial(exchange_kernel, n_seq, n_tx, peers),
        out_shape=(shape, shape),
        in_specs=[pl.BlockSpec(memory_space=pl.ANY)] * 2,
        out_specs=(pl.BlockSpec(memory_space=pl.ANY), pl.BlockSpec(memory_space=pl.ANY)),
        scratch_shapes=[
            pltpu.SemaphoreType.DMA((2, 9 * peers)),
            pltpu.SemaphoreType.DMA((2, chunks * peers)),
            pltpu.SemaphoreType.DMA((2,)),
        ],
        compiler_params=pltpu.CompilerParams(collective_id=0, has_side_effects=True),
    )(tok_send, grad_send)


def shards(tokens, grad_out, expert_ids, route_weights, gate_weight, up_weight, down_weight):
    expert_count = lax.axis_size("expert")
    seq_count = lax.axis_size("seq")
    tensor_count = lax.axis_size("tx") * lax.axis_size("core")
    core = lax.axis_index("core")
    local_count = gate_weight.shape[0]
    tok_rows = tokens.shape[0]
    model_width = tokens.shape[1]
    part_width = model_width // tensor_count
    per_peer = tok_rows // 6
    peer_count = expert_count * seq_count
    block_rows = local_count * per_peer
    slot_count = peer_count * block_rows
    flat_ids = expert_ids.reshape(-1)
    route_count = flat_ids.shape[0]
    onehot = (
        flat_ids[:, None] == jnp.arange(local_count * expert_count, dtype=jnp.int32)[None, :]
    ).astype(jnp.int32)
    before = jnp.cumsum(onehot, axis=0) - onehot
    ranking = jnp.sum(before * onehot, axis=1)
    local_expert = flat_ids % local_count
    dest_peer = flat_ids // local_count * seq_count + ranking % seq_count
    target = (dest_peer * local_count + local_expert) * per_peer + ranking // seq_count
    source = (
        jnp.full((slot_count,), -1, jnp.int32)
        .at[target]
        .set(jnp.arange(route_count, dtype=jnp.int32))
    )
    filled = source >= 0
    safe_source = jnp.maximum(source, 0)
    token_of = safe_source // 2
    weight_send = (
        route_weights.reshape(-1)[safe_source] * filled.astype(route_weights.dtype)
    ).reshape(peer_count, block_rows)
    own_part = lax.axis_index("tx") * 2 + core
    half = part_width
    tokens_half = lax.dynamic_slice_in_dim(tokens, own_part * half, half, axis=1)
    grad_half = lax.dynamic_slice_in_dim(grad_out, own_part * half, half, axis=1)
    tok_send = tokens_half[token_of].reshape(peer_count, block_rows, half)
    grad_send = grad_half[token_of].reshape(peer_count, block_rows, half)

    def join_halves(mine):
        both = jnp.broadcast_to(mine[None], (2,) + mine.shape)
        return lax.all_to_all(both, "core", split_axis=0, concat_axis=0, tiled=True)

    def by_expert(values):
        shaped = values.reshape((peer_count, local_count, per_peer) + values.shape[2:])
        return jnp.swapaxes(shaped, 0, 1).reshape(
            (local_count, peer_count * per_peer) + values.shape[2:]
        )

    def by_peer(values):
        shaped = values.reshape((local_count, peer_count, per_peer) + values.shape[2:])
        return jnp.swapaxes(shaped, 0, 1).reshape((peer_count, block_rows) + values.shape[2:])

    tok_recv, grad_recv = exchange_rows(tok_send, grad_send, seq_count, lax.axis_size("tx"))
    weight_send, tok_recv = lax.optimization_barrier((weight_send, tok_recv))
    weight_recv = lax.all_to_all(
        weight_send, ("expert", "seq"), split_axis=0, concat_axis=0, tiled=True
    )
    in_rows = jax.vmap(by_expert)(tok_recv)
    out_rows = jax.vmap(by_expert)(grad_recv)
    prob = by_expert(weight_recv).astype(jnp.float32)[:, :, None]
    weights = lax.all_gather(
        jnp.stack([gate_weight, up_weight, down_weight]), "seq", axis=2, tiled=True
    )
    gate_full, up_full, down_full = weights[0], weights[1], weights[2]
    hidden_count = gate_full.shape[2]
    gate_h, up_h, down_h = (
        w.reshape(local_count, tensor_count, half, hidden_count)
        for w in (gate_full, up_full, down_full)
    )
    pre_gate = jnp.einsum("cemd,ecdf->emf", in_rows, gate_h, preferred_element_type=jnp.float32)
    pre_up = jnp.einsum("cemd,ecdf->emf", in_rows, up_h, preferred_element_type=jnp.float32)
    sigmoid_gate = jax.nn.sigmoid(pre_gate)
    silu_gate = pre_gate * sigmoid_gate
    hidden = silu_gate * pre_up
    hidden_low = hidden.astype(jnp.bfloat16)
    back_proj = jnp.einsum("cemd,ecdf->emf", out_rows, down_h, preferred_element_type=jnp.float32)
    partial_scores = jnp.sum(hidden * back_proj, axis=2)
    scaled = (prob[None] * out_rows.astype(jnp.float32)).astype(jnp.bfloat16)
    hidden_grad = prob * back_proj
    up_grad = (hidden_grad * silu_gate).astype(jnp.bfloat16)
    gate_grad = (
        hidden_grad * pre_up * sigmoid_gate * (1.0 + pre_gate * (1.0 - sigmoid_gate))
    ).astype(jnp.bfloat16)
    gate_part = jnp.einsum("cemd,emf->ecdf", in_rows, gate_grad, preferred_element_type=jnp.float32)
    up_part = jnp.einsum("cemd,emf->ecdf", in_rows, up_grad, preferred_element_type=jnp.float32)
    down_part = jnp.einsum("cemd,emf->ecdf", scaled, hidden_low, preferred_element_type=jnp.float32)
    parts = jnp.stack([gate_part, up_part, down_part]).reshape(
        3, local_count, model_width, hidden_count
    ).astype(jnp.bfloat16)
    parts, gate_grad, up_grad = lax.optimization_barrier((parts, gate_grad, up_grad))
    reduced_parts = lax.psum_scatter(parts, "seq", scatter_dimension=2, tiled=True).astype(jnp.float32)
    grad_gate, grad_up, grad_down = reduced_parts[0], reduced_parts[1], reduced_parts[2]
    score_pad = 16
    gate_p, up_p = (
        jnp.pad(w, ((0, 0), (0, 0), (0, score_pad), (0, 0))) for w in (gate_h, up_h)
    )
    input_terms = jnp.einsum(
        "emf,ecdf->ecdm", gate_grad, gate_p, preferred_element_type=jnp.float32
    )
    input_terms = input_terms + jnp.einsum(
        "emf,ecdf->ecdm", up_grad, up_p, preferred_element_type=jnp.float32
    )
    input_terms = input_terms.at[:, :, part_width, :].set(partial_scores[:, None, :])
    rows_here = local_count * slot_count
    stacked = jnp.swapaxes(
        input_terms.reshape(local_count, tensor_count, part_width + score_pad, slot_count), 0, 1
    ).reshape(tensor_count, part_width + score_pad, rows_here).astype(jnp.bfloat16)
    tx_count = lax.axis_size("tx")
    stacked = stacked.reshape(tx_count, 2, part_width + score_pad, rows_here)
    pair = lax.all_to_all(stacked, "core", split_axis=1, concat_axis=1, tiled=True)
    pair = jnp.sum(pair.astype(jnp.float32), axis=1).astype(jnp.bfloat16)
    ring = lax.all_to_all(pair, "tx", split_axis=0, concat_axis=0, tiled=True)
    reduced = jnp.sum(ring.astype(jnp.float32), axis=0).astype(jnp.bfloat16)
    back_send = by_peer(
        jnp.swapaxes(reduced, 0, 1).reshape(local_count, slot_count, part_width + score_pad)
    )
    back_all = lax.all_to_all(
        back_send, ("expert", "seq"), split_axis=0, concat_axis=0, tiled=True
    ).astype(jnp.float32)
    back_all = back_all.reshape(slot_count, part_width + score_pad)[target]
    route_rows = back_all[:, :part_width].reshape(tok_rows, 2, part_width)
    grad_tokens = jnp.sum(route_rows, axis=1).astype(jnp.bfloat16)
    grad_route = back_all[:, part_width].reshape(tok_rows, 2)
    return (grad_tokens, grad_route, grad_gate, grad_up, grad_down)


def solution(mesh):
    shape = mesh.devices.shape
    mesh = jax.sharding.Mesh(
        mesh.devices.reshape(shape[0], shape[1], shape[2] // 2, 2), ("expert", "seq", "tx", "core")
    )
    tensor = ("tx", "core")
    placed = (
        P(("expert", "seq"), None),
        P(("expert", "seq"), None),
        P(("expert", "seq"), None),
        P(("expert", "seq"), None),
        P("expert", "seq", tensor),
        P("expert", "seq", tensor),
        P("expert", "seq", tensor),
    )
    return jax.shard_map(
        shards,
        mesh=mesh,
        in_specs=placed,
        out_specs=(
            P(("expert", "seq"), tensor),
            P(("expert", "seq"), None),
            P("expert", "seq", tensor),
            P("expert", "seq", tensor),
            P("expert", "seq", tensor),
        ),
        check_vma=False,
    )
```

profile of v0, /device:TPU:0, one launch (start us, length us, event | category | flops | bytes accessed | tf_op | source)
XLA Modules:
  0.0 351.1 jit_solution(6700158249557075205)
XLA Ops:
  7.2 3.5 %pad_maximum_fusion.1 = bf16[3,1,1792,256]{3,2,1,0:T(8,128)(2,1)} fusion(bf16[1,1,1792,256]{3,2,1,0:T(8,128)(2,1)} %bitcast.119, bf16[1,1,1792,256]{3,2,1,0:T(8,128)(2,1)} %bitcast.120, bf16[1,1,1792,256]{3,2,1,0:T(8,128)(2,1)} %bitcast.121), kind=kLoop, calls=%fused_computation.19 | loop fusion | flops 2752512 | bytes 5505024 | tf_op jit(solution)/shard_map/stack | solution.py:215
  13.6 2.9 scatter_custom_fusion
  16.6 3.5 %gather_fusion = bf16[512]{0:T(512)(128)(2,1)S(1)} fusion(bf16[384]{0:T(512)(128)(2,1)S(1)} %reshape.379, s32[1024]{0:T(1024)S(1)} %get-tuple-element.75), kind=kCustom, calls=%fused_computation | custom fusion | bytes 4096 | tf_op jit(solution)/shard_map/gather | solution.py:183
  21.3 2.7 gather_fusion.2
  24.1 2.7 gather_fusion.1
  26.8 114.1 %shard_map.110 = (bf16[8,16,32,896]{3,2,1,0:T(8,128)(2,1)}, bf16[8,16,32,896]{3,2,1,0:T(8,128)(2,1)}) custom-call(bf16[16,32,896]{2,1,0:T(8,128)(2,1)} %bitcast.115, bf16[16,32,896]{2,1,0:T(8,128)(2,1)} %bitcast.114), custom_call_target="tpu_custom_call" | custom-call | tf_op jit(solution)/shard_map/pallas_call | solution.py:137
  141.5 4.2 %all-to-all-start = ((bf16[16,1,32]{2,1,0:T(2,128)(2,1)}), bf16[16,1,32]{2,1,0:T(2,128)(2,1)S(1)}, u32[]{:S(2)}, u32[]{:S(2)}) async-start(bf16[16,1,32]{2,1,0:T(2,128)(2,1)} %copy.74), calls=%async_computation | async-start | bytes 16384 | tf_op jit(solution)/shard_map/all_to_all | solution.py:208
  145.7 11.3 %copy.73 = bf16[8,512,896]{1,2,0:T(8,128)(2,1)} copy(bf16[8,512,896]{2,1,0:T(8,128)(2,1)} %bitcast.107) | data formatting | bytes 14680064 | tf_op jit(solution)/shard_map/reshape.60
  157.1 8.4 %multiply_convert_fusion = bf16[8,16,32,896]{3,2,1,0:T(8,128)(2,1)} fusion(bf16[8,16,32,896]{3,2,1,0:T(8,128)(2,1)} %get-tuple-element.27, f32[16,32]{1,0:T(8,128)S(1)} %bitcast.122), kind=kLoop, calls=%fused_computation.5 | loop fusion | flops 11010048 | bytes 14682112 | tf_op jit(solution)/shard_map/convert_element_type | solution.py:231
  165.5 11.2 %copy.78 = bf16[8,512,896]{1,2,0:T(8,128)(2,1)} copy(bf16[8,512,896]{2,1,0:T(8,128)(2,1)} %bitcast.99) | data formatting | bytes 14680064 | tf_op jit(solution)/shard_map/convert_element_type | solution.py:231
  176.7 4.8 %fusion.25 = (bf16[1,1,7168,256]{3,2,1,0:T(8,128)(2,1)S(1)}, bf16[1,1,7168,256]{3,2,1,0:T(8,128)(2,1)S(1)}, bf16[1,1,7168,256]{3,2,1,0:T(8,128)(2,1)S(1)}) fusion(bf16[3,1,7168,256]{3,2,1,0:T(8,128)(2,1)} %all-gather.2.cloned.1.call-done), kind=kLoop, calls=%fused_computation.72 | loop fusion | bytes 22020096 | tf_op jit(solution)/shard_map/slice | solution.py:217
  181.5 7.9 %convolution_bitcast_fusion = f32[512,256]{0,1:T(8,128)S(1)} fusion(bf16[8,512,896]{2,1,0:T(8,128)(2,1)} %bitcast.108, bf16[8,896,256]{2,1,0:T(8,128)(2,1)S(1)} %bitcast.102), kind=kOutput, calls=%fused_computation.23 | convolution fusion | flops 1879048192 | bytes 11534336 | tf_op jit(solution)/shard_map/cemd,ecdf->emf/dot_general | solution.py:223
  189.4 5.4 %convolution_bitcast_fusion.1 = f32[512,256]{0,1:T(8,128)S(1)} fusion(bf16[8,512,896]{2,1,0:T(8,128)(2,1)} %bitcast.109, bf16[8,896,256]{2,1,0:T(8,128)(2,1)S(1)} %bitcast.100), kind=kOutput, calls=%fused_computation.24 | convolution fusion | flops 1879048192 | bytes 11534336 | tf_op jit(solution)/shard_map/cemd,ecdf->emf/dot_general | solution.py:224
  194.9 2.3 multiply_reduce_fusion
  197.2 2.1 fusion.1
  199.3 2.1 fusion
  201.5 2.2 fusion.2
  203.7 5.2 %pad_maximum_fusion = bf16[3,1,7168,256]{3,2,1,0:T(8,128)(2,1)} fusion(bf16[1,1,7168,256]{3,2,1,0:T(8,128)(2,1)S(1)} %fusion.2, bf16[1,1,7168,256]{3,2,1,0:T(8,128)(2,1)S(1)} %fusion.1, bf16[1,1,7168,256]{3,2,1,0:T(8,128)(2,1)S(1)} %fusion), kind=kLoop, calls=%fused_computation.6 | loop fusion | flops 11010048 | bytes 22020096 | tf_op jit(solution)/shard_map/stack | solution.py:240
  208.9 9.6 %fusion.4 = f32[8,912,512]{2,1,0:T(8,128)} fusion(bf16[1,8,896,256]{3,2,1,0:T(8,128)(2,1)} %bitcast.103, bf16[1,512,256]{1,2,0:T(8,128)(2,1)S(1)} %bitcast.118), kind=kOutput, calls=%fused_computation.15 | convolution fusion | flops 1912602624 | bytes 18874368 | tf_op jit(solution)/shard_map/emf,ecdf->ecdm/dot_general | solution.py:250
  218.5 9.2 %convolution_add_fusion = bf16[8,912,512]{2,1,0:T(8,128)(2,1)} fusion(f32[8,912,512]{2,1,0:T(8,128)} %fusion.4, bf16[1,8,896,256]{3,2,1,0:T(8,128)(2,1)S(1)} %bitcast.101, bf16[1,512,256]{1,2,0:T(8,128)(2,1)S(1)} %bitcast.117), kind=kOutput, calls=%fused_computation.10 | convolution fusion | flops 1920073728 | bytes 26345472 | tf_op jit(solution)/shard_map/emf,ecdf->ecdm/dot_general | solution.py:253
  227.6 1.5 scatter.13
  229.2 3.7 %copy.81 = bf16[4,2,912,512]{3,2,0,1:T(8,128)(2,1)S(1)} copy(bf16[4,2,912,512]{3,2,1,0:T(8,128)(2,1)} %bitcast.98) | data formatting | bytes 14942208 | tf_op jit(solution)/shard_map/reshape | solution.py:262
  232.9 11.3 %all_to_all.24 = bf16[4,2,912,512]{3,2,0,1:T(8,128)(2,1)} all-to-all(bf16[4,2,912,512]{3,2,0,1:T(8,128)(2,1)S(1)} %copy.81), channel_id=1, replica_groups=mesh['expert'=4,'seq'=4,'tx'=4,'core'=2] {'core'}, dimensions={1} | all-to-all | bytes 14942208 | tf_op jit(solution)/shard_map/all_to_all | solution.py:263
  244.2 7.9 %reduce_sum.56 = bf16[4,912,512]{2,1,0:T(8,128)(2,1)} reduce(bf16[4,2,912,512]{3,2,0,1:T(8,128)(2,1)} %all_to_all.24, bf16[]{:T(256)} %constant.108.clone.1), dimensions={1}, to_apply=%region_5.6 | reduce | flops 1867776 | bytes 11206658 | tf_op jit(solution)/shard_map/reduce_sum | solution.py:264
  252.1 50.1 %all_to_all.25 = bf16[4,912,512]{2,1,0:T(8,128)(2,1)} all-to-all(bf16[4,912,512]{2,1,0:T(8,128)(2,1)} %reduce_sum.56), channel_id=1, replica_groups=mesh['expert'=4,'seq'=4,'tx'=4,'core'=2] {'tx'}, dimensions={0} | all-to-all | bytes 7471104 | tf_op jit(solution)/shard_map/all_to_all | solution.py:265
  302.1 3.2 reduce_sum.57
  306.7 6.9 %all-to-all-start.3 = ((bf16[16,32,912]{2,1,0:T(8,128)(2,1)}), bf16[16,32,912]{2,1,0:T(8,128)(2,1)S(1)}, u32[]{:S(2)}, u32[]{:S(2)}) async-start(bf16[16,32,912]{2,1,0:T(8,128)(2,1)} %bitcast.37), calls=%async_computation.3 | async-start | bytes 2097152 | tf_op jit(solution)/shard_map/all_to_all | solution.py:270
  313.6 16.4 %all-to-all-done.3 = bf16[16,32,912]{2,1,0:T(8,128)(2,1)S(1)} async-done(((bf16[16,32,912]{2,1,0:T(8,128)(2,1)}), bf16[16,32,912]{2,1,0:T(8,128)(2,1)S(1)}, u32[]{:S(2)}, u32[]{:S(2)}) %all-to-all-start.3) | async-done | bytes 933920 | tf_op jit(solution)/shard_map/all_to_all | solution.py:270
  330.3 2.5 gather_fusion.3
  337.0 2.5 reduce_sum.58
  339.5 2.2 convert_element_type.103
  341.7 2.6 slice_bitcast_fusion
  (66 shorter events, 10.6 us)
Async XLA Ops:
  7.2 169.5 %all-gather.2.cloned.1.call-start = ((), (), s32[]{:S(2)}) async-start(), calls=%async_computation.5 | async-start | bytes 13762560 | tf_op jit(solution)/shard_map/all_gather | solution.py:214
  7.2 3.6 %copy-start.3 = (s32[192,2]{0,1:T(2,128)S(1)}, s32[192,2]{0,1:T(2,128)}, u32[]{:S(2)}) copy-start(s32[192,2]{0,1:T(2,128)} %param.11) | copy-start | bytes 4612
  7.2 4.0 %copy-start.4 = (bf16[192,2]{0,1:T(2,128)(2,1)S(1)}, bf16[192,2]{0,1:T(2,128)(2,1)}, u32[]{:S(2)}) copy-start(bf16[192,2]{0,1:T(2,128)(2,1)} %param.12) | copy-start | bytes 2308
  141.5 15.5 %all-to-all-start = ((bf16[16,1,32]{2,1,0:T(2,128)(2,1)}), bf16[16,1,32]{2,1,0:T(2,128)(2,1)S(1)}, u32[]{:S(2)}, u32[]{:S(2)}) async-start(bf16[16,1,32]{2,1,0:T(2,128)(2,1)} %copy.74), calls=%async_computation | async-start | bytes 16384 | tf_op jit(solution)/shard_map/all_to_all | solution.py:208
  145.7 193.8 %reduce-scatter.2.cloned.1.call-start = ((), (), s32[]{:S(2)}) async-start(), calls=%async_computation.6 | async-start | bytes 13762560 | tf_op jit(solution)/shard_map/reduce_scatter | solution.py:244
  181.4 7.9 %copy-start.2 = (bf16[1,1,7168,256]{3,2,1,0:T(8,128)(2,1)}, bf16[1,1,7168,256]{3,2,1,0:T(8,128)(2,1)S(1)}, u32[]{:S(2)}) copy-start(bf16[1,1,7168,256]{3,2,1,0:T(8,128)(2,1)S(1)} %get-tuple-element.63) | copy-start | bytes 11010052
  181.5 7.9 %copy-start = (bf16[1,1,7168,256]{3,2,1,0:T(8,128)(2,1)}, bf16[1,1,7168,256]{3,2,1,0:T(8,128)(2,1)S(1)}, u32[]{:S(2)}) copy-start(bf16[1,1,7168,256]{3,2,1,0:T(8,128)(2,1)S(1)} %get-tuple-element.62) | copy-start | bytes 11010052
  181.5 13.4 %slice-start.2 = ((s8[7340032]{0:T(1024)(128)(4,1)}), s8[4194304]{0:T(1024)(128)(4,1)S(1)}, s32[]{:S(2)}) async-start(s8[7340032]{0:T(1024)(128)(4,1)} %bitcast.104), calls=%async_computation.9 | async-start | bytes 8388608
  189.4 5.4 %slice-start.3 = ((s8[7340032]{0:T(1024)(128)(4,1)}), s8[3145728]{0:T(1024)(128)(4,1)S(1)}, s32[]{:S(2)}) async-start(s8[7340032]{0:T(1024)(128)(4,1)} %bitcast.104), calls=%async_computation.10 | async-start | bytes 6291456
  189.4 7.8 %slice-start = ((s8[7340032]{0:T(1024)(128)(4,1)}), s8[4194304]{0:T(1024)(128)(4,1)S(1)}, s32[]{:S(2)}) async-start(s8[7340032]{0:T(1024)(128)(4,1)} %bitcast.94), calls=%async_computation.7 | async-start | bytes 8388608
  194.9 2.3 slice-start.1
  197.2 4.2 %slice-start.4 = ((s8[7340032]{0:T(1024)(128)(4,1)}), s8[4194304]{0:T(1024)(128)(4,1)S(1)}, s32[]{:S(2)}) async-start(s8[7340032]{0:T(1024)(128)(4,1)} %bitcast.110), calls=%async_computation.11 | async-start | bytes 8388608
  199.3 2.1 slice-start.5
  208.9 9.6 %copy-start.1 = (bf16[1,1,7168,256]{3,2,1,0:T(8,128)(2,1)S(1)}, bf16[1,1,7168,256]{3,2,1,0:T(8,128)(2,1)}, u32[]{:S(2)}) copy-start(bf16[1,1,7168,256]{3,2,1,0:T(8,128)(2,1)} %copy-done) | copy-start | bytes 11010052
  306.7 23.4 %all-to-all-start.3 = ((bf16[16,32,912]{2,1,0:T(8,128)(2,1)}), bf16[16,32,912]{2,1,0:T(8,128)(2,1)S(1)}, u32[]{:S(2)}, u32[]{:S(2)}) async-start(bf16[16,32,912]{2,1,0:T(8,128)(2,1)} %bitcast.37), calls=%async_computation.3 | async-start | bytes 2097152 | tf_op jit(solution)/shard_map/all_to_all | solution.py:270
Sparse Core Ops, SparseCore 0:
  10.9 127.4 all-gather.1
  209.0 103.3 reduce-scatter.1
where the time goes:
time: 352 us; the launch traced here: 351 us
  Pallas kernels  114 us (32%)
  blocking collectives  61.4 us (17%)
  local copies, waits for them, and re-layouts  57.9 us (16%)
  matrix products  40.7 us (12%)
  other arithmetic  34.9 us (10%)
  waiting for transfers between devices  16.5 us (5%)
  between operations  14.5 us (4%)
  starting transfers between devices  11.2 us (3%)
    pallas_call x1, Pallas kernels, exchange_rows(): pl.pallas_call(functools.partial(exchange_kernel, n_seq, n_tx, peers), ou...  114 us
    all_to_all x1, blocking collectives, shards(): ring = lax.all_to_all(pair, 'tx', split_axis=0, concat_axis=0, tiled=True)  50.1 us
    all_to_all x1, waiting for transfers between devices, shards(): lax.all_to_all(back_send, ('expert', 'seq'), split_axis=0, concat_axis=0,...  16.4 us
    another operation x2, local copies, waits for them, and re-layouts  11.5 us
    all_to_all x1, blocking collectives, shards(): lax.all_to_all(stacked, 'core', split_axis=1, concat_axis=1, tiled=True)  11.3 us
    convert_element_type x1, local copies, waits for them, and re-layouts, shards(): scaled = (prob[None] * out_rows.astype(jnp.float32)).astype(jnp.bfloat16)  11.2 us
    dot_general x1, matrix products, shards(): jnp.einsum('emf,ecdf->ecdm', gate_grad, gate_p, preferred_element_type=jn...  9.57 us
    dot_general x1, matrix products, shards(): jnp.einsum('emf,ecdf->ecdm', up_grad, up_p, preferred_element_type=jnp.fl...  9.16 us
  transfers between devices with their start and end apart: 4, of which 1 were waited for; matrix products, arithmetic and copies ran while one was open for 27% of the time, Pallas kernels for 32%

commit v1 on v0

--- a/solution.py
+++ b/solution.py
@@ -241,8 +241,8 @@
         3, local_count, model_width, hidden_count
     ).astype(jnp.bfloat16)
     parts, gate_grad, up_grad = lax.optimization_barrier((parts, gate_grad, up_grad))
-    reduced_parts = lax.psum_scatter(parts, "seq", scatter_dimension=2, tiled=True).astype(jnp.float32)
-    grad_gate, grad_up, grad_down = reduced_parts[0], reduced_parts[1], reduced_parts[2]
+    reduced_parts = lax.psum_scatter(parts, "seq", scatter_dimension=2, tiled=True)
+    grad_gate, grad_up, grad_down = (reduced_parts[w].astype(jnp.float32) for w in range(3))
     score_pad = 16
     gate_p, up_p = (
         jnp.pad(w, ((0, 0), (0, 0), (0, score_pad), (0, 0))) for w in (gate_h, up_h)

time: 352 us -> 353 us (level)
  transfers between devices with their start and end apart: 4 -> 4, of which waited for: 1 -> 1; matrix products, arithmetic and copies ran while one was open for 27% -> 26% of each run, Pallas kernels for 32% -> 32%
where the time goes in v1:
time: 353 us; the launch traced here: 352 us
  Pallas kernels  114 us (32%)
  blocking collectives  61.4 us (17%)
  local copies, waits for them, and re-layouts  55.4 us (16%)
  matrix products  40.7 us (12%)
  other arithmetic  38.2 us (11%)
  waiting for transfers between devices  16.5 us (5%)
  between operations  14.5 us (4%)
  starting transfers between devices  11.2 us (3%)
    pallas_call x1, Pallas kernels, exchange_rows(): pl.pallas_call(functools.partial(exchange_kernel, n_seq, n_tx, peers), ou...  114 us
    all_to_all x1, blocking collectives, shards(): ring = lax.all_to_all(pair, 'tx', split_axis=0, concat_axis=0, tiled=True)  50.1 us
    all_to_all x1, waiting for transfers between devices, shards(): lax.all_to_all(back_send, ('expert', 'seq'), split_axis=0, concat_axis=0,...  16.4 us
    another operation x2, local copies, waits for them, and re-layouts  11.5 us
    all_to_all x1, blocking collectives, shards(): lax.all_to_all(stacked, 'core', split_axis=1, concat_axis=1, tiled=True)  11.3 us
    convert_element_type x1, local copies, waits for them, and re-layouts, shards(): scaled = (prob[None] * out_rows.astype(jnp.float32)).astype(jnp.bfloat16)  11.2 us
    dot_general x1, matrix products, shards(): jnp.einsum('emf,ecdf->ecdm', gate_grad, gate_p, preferred_element_type=jn...  9.57 us
    dot_general x1, matrix products, shards(): jnp.einsum('emf,ecdf->ecdm', up_grad, up_p, preferred_element_type=jnp.fl...  9.16 us
  transfers between devices with their start and end apart: 4, of which 1 were waited for; matrix products, arithmetic and copies ran while one was open for 26% of the time, Pallas kernels for 32%

profile of v1, /device:TPU:0, one launch (start us, length us, event | category | flops | bytes accessed | tf_op | source)
XLA Modules:
  0.0 351.9 jit_solution(12649907452761985445)
XLA Ops:
  7.2 3.5 %pad_maximum_fusion.1 = bf16[3,1,1792,256]{3,2,1,0:T(8,128)(2,1)} fusion(bf16[1,1,1792,256]{3,2,1,0:T(8,128)(2,1)} %bitcast.128, bf16[1,1,1792,256]{3,2,1,0:T(8,128)(2,1)} %bitcast.129, bf16[1,1,1792,256]{3,2,1,0:T(8,128)(2,1)} %bitcast.130), kind=kLoop, calls=%fused_computation.19 | loop fusion | flops 2752512 | bytes 5505024 | tf_op jit(solution)/shard_map/stack | solution.py:215
  13.6 2.9 scatter_custom_fusion
  16.6 3.5 gather_fusion
  21.3 2.7 gather_fusion.2
  24.1 2.7 gather_fusion.1
  26.8 114.1 %shard_map.110 = (bf16[8,16,32,896]{3,2,1,0:T(8,128)(2,1)}, bf16[8,16,32,896]{3,2,1,0:T(8,128)(2,1)}) custom-call(bf16[16,32,896]{2,1,0:T(8,128)(2,1)} %bitcast.124, bf16[16,32,896]{2,1,0:T(8,128)(2,1)} %bitcast.123), custom_call_target="tpu_custom_call" | custom-call | tf_op jit(solution)/shard_map/pallas_call | solution.py:137
  141.5 4.2 %all-to-all-start = ((bf16[16,1,32]{2,1,0:T(2,128)(2,1)}), bf16[16,1,32]{2,1,0:T(2,128)(2,1)S(1)}, u32[]{:S(2)}, u32[]{:S(2)}) async-start(bf16[16,1,32]{2,1,0:T(2,128)(2,1)} %copy.74), calls=%async_computation | async-start | bytes 16384 | tf_op jit(solution)/shard_map/all_to_all | solution.py:208
  145.7 11.3 %copy.73 = bf16[8,512,896]{1,2,0:T(8,128)(2,1)} copy(bf16[8,512,896]{2,1,0:T(8,128)(2,1)} %bitcast.116) | data formatting | bytes 14680064 | tf_op jit(solution)/shard_map/reshape.60
  157.1 8.4 %multiply_convert_fusion = bf16[8,16,32,896]{3,2,1,0:T(8,128)(2,1)} fusion(bf16[8,16,32,896]{3,2,1,0:T(8,128)(2,1)} %get-tuple-element.27, f32[16,32]{1,0:T(8,128)S(1)} %bitcast.131), kind=kLoop, calls=%fused_computation.5 | loop fusion | flops 11010048 | bytes 14682112 | tf_op jit(solution)/shard_map/convert_element_type | solution.py:231
  165.5 11.2 %copy.78 = bf16[8,512,896]{1,2,0:T(8,128)(2,1)} copy(bf16[8,512,896]{2,1,0:T(8,128)(2,1)} %bitcast.108) | data formatting | bytes 14680064 | tf_op jit(solution)/shard_map/convert_element_type | solution.py:231
  176.7 4.8 %fusion.28 = (bf16[1,1,7168,256]{3,2,1,0:T(8,128)(2,1)S(1)}, bf16[1,1,7168,256]{3,2,1,0:T(8,128)(2,1)S(1)}, bf16[1,1,7168,256]{3,2,1,0:T(8,128)(2,1)S(1)}) fusion(bf16[3,1,7168,256]{3,2,1,0:T(8,128)(2,1)} %all-gather.2.cloned.1.call-done), kind=kLoop, calls=%fused_computation.75 | loop fusion | bytes 22020096 | tf_op jit(solution)/shard_map/slice | solution.py:217
  181.5 7.9 %convolution_bitcast_fusion = f32[512,256]{0,1:T(8,128)S(1)} fusion(bf16[8,512,896]{2,1,0:T(8,128)(2,1)} %bitcast.117, bf16[8,896,256]{2,1,0:T(8,128)(2,1)S(1)} %bitcast.111), kind=kOutput, calls=%fused_computation.20 | convolution fusion | flops 1879048192 | bytes 11534336 | tf_op jit(solution)/shard_map/cemd,ecdf->emf/dot_general | solution.py:223
  189.4 5.4 %convolution_bitcast_fusion.1 = f32[512,256]{0,1:T(8,128)S(1)} fusion(bf16[8,512,896]{2,1,0:T(8,128)(2,1)} %bitcast.118, bf16[8,896,256]{2,1,0:T(8,128)(2,1)S(1)} %bitcast.109), kind=kOutput, calls=%fused_computation.21 | convolution fusion | flops 1879048192 | bytes 11534336 | tf_op jit(solution)/shard_map/cemd,ecdf->emf/dot_general | solution.py:224
  194.9 2.3 multiply_reduce_fusion
  197.2 2.1 fusion.1
  199.3 2.1 fusion
  201.5 2.2 fusion.2
  203.7 5.2 %pad_maximum_fusion = bf16[3,1,7168,256]{3,2,1,0:T(8,128)(2,1)} fusion(bf16[1,1,7168,256]{3,2,1,0:T(8,128)(2,1)S(1)} %fusion.2, bf16[1,1,7168,256]{3,2,1,0:T(8,128)(2,1)S(1)} %fusion.1, bf16[1,1,7168,256]{3,2,1,0:T(8,128)(2,1)S(1)} %fusion), kind=kLoop, calls=%fused_computation.6 | loop fusion | flops 11010048 | bytes 22020096 | tf_op jit(solution)/shard_map/stack | solution.py:240
  208.9 9.6 %fusion.4 = f32[8,912,512]{2,1,0:T(8,128)} fusion(bf16[1,8,896,256]{3,2,1,0:T(8,128)(2,1)} %bitcast.112, bf16[1,512,256]{1,2,0:T(8,128)(2,1)S(1)} %bitcast.127), kind=kOutput, calls=%fused_computation.15 | convolution fusion | flops 1912602624 | bytes 18874368 | tf_op jit(solution)/shard_map/emf,ecdf->ecdm/dot_general | solution.py:250
  218.5 9.2 %convolution_add_fusion = bf16[8,912,512]{2,1,0:T(8,128)(2,1)} fusion(f32[8,912,512]{2,1,0:T(8,128)} %fusion.4, bf16[1,8,896,256]{3,2,1,0:T(8,128)(2,1)S(1)} %bitcast.110, bf16[1,512,256]{1,2,0:T(8,128)(2,1)S(1)} %bitcast.126), kind=kOutput, calls=%fused_computation.10 | convolution fusion | flops 1920073728 | bytes 26345472 | tf_op jit(solution)/shard_map/emf,ecdf->ecdm/dot_general | solution.py:253
  227.6 1.5 scatter.13
  229.2 3.7 %copy.81 = bf16[4,2,912,512]{3,2,0,1:T(8,128)(2,1)S(1)} copy(bf16[4,2,912,512]{3,2,1,0:T(8,128)(2,1)} %bitcast.107) | data formatting | bytes 14942208 | tf_op jit(solution)/shard_map/reshape | solution.py:262
  232.9 11.3 %all_to_all.24 = bf16[4,2,912,512]{3,2,0,1:T(8,128)(2,1)} all-to-all(bf16[4,2,912,512]{3,2,0,1:T(8,128)(2,1)S(1)} %copy.81), channel_id=1, replica_groups=mesh['expert'=4,'seq'=4,'tx'=4,'core'=2] {'core'}, dimensions={1} | all-to-all | bytes 14942208 | tf_op jit(solution)/shard_map/all_to_all | solution.py:263
  244.2 7.9 %reduce_sum.56 = bf16[4,912,512]{2,1,0:T(8,128)(2,1)} reduce(bf16[4,2,912,512]{3,2,0,1:T(8,128)(2,1)} %all_to_all.24, bf16[]{:T(256)} %constant.108.clone.1), dimensions={1}, to_apply=%region_5.6 | reduce | flops 1867776 | bytes 11206658 | tf_op jit(solution)/shard_map/reduce_sum | solution.py:264
  252.1 50.1 %all_to_all.25 = bf16[4,912,512]{2,1,0:T(8,128)(2,1)} all-to-all(bf16[4,912,512]{2,1,0:T(8,128)(2,1)} %reduce_sum.56), channel_id=1, replica_groups=mesh['expert'=4,'seq'=4,'tx'=4,'core'=2] {'tx'}, dimensions={0} | all-to-all | bytes 7471104 | tf_op jit(solution)/shard_map/all_to_all | solution.py:265
  302.1 3.2 reduce_sum.57
  306.7 6.9 %all-to-all-start.3 = ((bf16[16,32,912]{2,1,0:T(8,128)(2,1)}), bf16[16,32,912]{2,1,0:T(8,128)(2,1)S(1)}, u32[]{:S(2)}, u32[]{:S(2)}) async-start(bf16[16,32,912]{2,1,0:T(8,128)(2,1)} %bitcast.37), calls=%async_computation.3 | async-start | bytes 2097152 | tf_op jit(solution)/shard_map/all_to_all | solution.py:270
  313.6 16.4 %all-to-all-done.3 = bf16[16,32,912]{2,1,0:T(8,128)(2,1)S(1)} async-done(((bf16[16,32,912]{2,1,0:T(8,128)(2,1)}), bf16[16,32,912]{2,1,0:T(8,128)(2,1)S(1)}, u32[]{:S(2)}, u32[]{:S(2)}) %all-to-all-start.3) | async-done | bytes 933920 | tf_op jit(solution)/shard_map/all_to_all | solution.py:270
  330.3 2.5 gather_fusion.3
  334.2 1.9 reshape.438
  337.0 3.7 %reduce_sum.58 = bf16[192,896]{1,0:T(8,128)(2,1)} reduce(f32[192,2,896]{2,1,0:T(2,128)} %reshape.438, f32[]{:T(128)} %constant.123.clone.1), dimensions={1}, to_apply=%region_7.8 | reduce | flops 172032 | bytes 1720324 | tf_op jit(solution)/shard_map/reduce_sum | solution.py:275
  340.7 4.3 %fusion.8 = (f32[1,1792,256]{2,1,0:T(8,128)}, f32[1,1792,256]{2,1,0:T(8,128)}, f32[1,1792,256]{2,1,0:T(8,128)}) fusion(bf16[3,1,1792,256]{3,2,1,0:T(8,128)(2,1)} %reduce-scatter.2.cloned.1.call-done), kind=kLoop, calls=%fused_computation.25 | loop fusion | flops 1376256 | bytes 8257536 | tf_op jit(solution)/shard_map/convert_element_type | solution.py:245
  (68 shorter events, 8.8 us)
Async XLA Ops:
  7.2 169.5 %all-gather.2.cloned.1.call-start = ((), (), s32[]{:S(2)}) async-start(), calls=%async_computation.5 | async-start | bytes 13762560 | tf_op jit(solution)/shard_map/all_gather | solution.py:214
  7.2 3.6 %copy-start.4 = (s32[192,2]{0,1:T(2,128)S(1)}, s32[192,2]{0,1:T(2,128)}, u32[]{:S(2)}) copy-start(s32[192,2]{0,1:T(2,128)} %param.11) | copy-start | bytes 4612
  7.2 4.0 %copy-start.5 = (bf16[192,2]{0,1:T(2,128)(2,1)S(1)}, bf16[192,2]{0,1:T(2,128)(2,1)}, u32[]{:S(2)}) copy-start(bf16[192,2]{0,1:T(2,128)(2,1)} %param.12) | copy-start | bytes 2308
  141.5 15.5 %all-to-all-start = ((bf16[16,1,32]{2,1,0:T(2,128)(2,1)}), bf16[16,1,32]{2,1,0:T(2,128)(2,1)S(1)}, u32[]{:S(2)}, u32[]{:S(2)}) async-start(bf16[16,1,32]{2,1,0:T(2,128)(2,1)} %copy.74), calls=%async_computation | async-start | bytes 16384 | tf_op jit(solution)/shard_map/all_to_all | solution.py:208
  145.7 195.1 %reduce-scatter.2.cloned.1.call-start = ((), (), s32[]{:S(2)}) async-start(), calls=%async_computation.6 | async-start | bytes 13762560 | tf_op jit(solution)/shard_map/reduce_scatter | solution.py:244
  181.4 7.9 %copy-start.2 = (bf16[1,1,7168,256]{3,2,1,0:T(8,128)(2,1)}, bf16[1,1,7168,256]{3,2,1,0:T(8,128)(2,1)S(1)}, u32[]{:S(2)}) copy-start(bf16[1,1,7168,256]{3,2,1,0:T(8,128)(2,1)S(1)} %get-tuple-element.63) | copy-start | bytes 11010052
  181.5 7.9 %copy-start = (bf16[1,1,7168,256]{3,2,1,0:T(8,128)(2,1)}, bf16[1,1,7168,256]{3,2,1,0:T(8,128)(2,1)S(1)}, u32[]{:S(2)}) copy-start(bf16[1,1,7168,256]{3,2,1,0:T(8,128)(2,1)S(1)} %get-tuple-element.62) | copy-start | bytes 11010052
  181.5 13.4 %slice-start.2 = ((s8[7340032]{0:T(1024)(128)(4,1)}), s8[4194304]{0:T(1024)(128)(4,1)S(1)}, s32[]{:S(2)}) async-start(s8[7340032]{0:T(1024)(128)(4,1)} %bitcast.113), calls=%async_computation.9 | async-start | bytes 8388608
  189.4 5.4 %slice-start.3 = ((s8[7340032]{0:T(1024)(128)(4,1)}), s8[3145728]{0:T(1024)(128)(4,1)S(1)}, s32[]{:S(2)}) async-start(s8[7340032]{0:T(1024)(128)(4,1)} %bitcast.113), calls=%async_computation.10 | async-start | bytes 6291456
  189.4 7.8 %slice-start = ((s8[7340032]{0:T(1024)(128)(4,1)}), s8[4194304]{0:T(1024)(128)(4,1)S(1)}, s32[]{:S(2)}) async-start(s8[7340032]{0:T(1024)(128)(4,1)} %bitcast.103), calls=%async_computation.7 | async-start | bytes 8388608
  194.9 2.3 slice-start.1
  197.2 4.2 %slice-start.4 = ((s8[7340032]{0:T(1024)(128)(4,1)}), s8[4194304]{0:T(1024)(128)(4,1)S(1)}, s32[]{:S(2)}) async-start(s8[7340032]{0:T(1024)(128)(4,1)} %bitcast.119), calls=%async_computation.11 | async-start | bytes 8388608
  199.3 2.1 slice-start.5
  208.9 9.6 %copy-start.1 = (bf16[1,1,7168,256]{3,2,1,0:T(8,128)(2,1)S(1)}, bf16[1,1,7168,256]{3,2,1,0:T(8,128)(2,1)}, u32[]{:S(2)}) copy-start(bf16[1,1,7168,256]{3,2,1,0:T(8,128)(2,1)} %copy-done) | copy-start | bytes 11010052
  306.7 23.4 %all-to-all-start.3 = ((bf16[16,32,912]{2,1,0:T(8,128)(2,1)}), bf16[16,32,912]{2,1,0:T(8,128)(2,1)S(1)}, u32[]{:S(2)}, u32[]{:S(2)}) async-start(bf16[16,32,912]{2,1,0:T(8,128)(2,1)} %bitcast.37), calls=%async_computation.3 | async-start | bytes 2097152 | tf_op jit(solution)/shard_map/all_to_all | solution.py:270
  332.8 1.3 slice-start.6
  332.8 3.2 copy-start.3
Sparse Core Ops, SparseCore 0:
  10.9 127.4 all-gather.1
  209.0 103.3 reduce-scatter.1

commit v2 on v0

--- a/solution.py
+++ b/solution.py
@@ -270,10 +270,11 @@
     back_all = lax.all_to_all(
         back_send, ("expert", "seq"), split_axis=0, concat_axis=0, tiled=True
     ).astype(jnp.float32)
-    back_all = back_all.reshape(slot_count, part_width + score_pad)[target]
-    route_rows = back_all[:, :part_width].reshape(tok_rows, 2, part_width)
-    grad_tokens = jnp.sum(route_rows, axis=1).astype(jnp.bfloat16)
-    grad_route = back_all[:, part_width].reshape(tok_rows, 2)
+    back_all = back_all.reshape(slot_count, part_width + score_pad)
+    pair_target = target.reshape(tok_rows, 2)
+    first, second = back_all[pair_target[:, 0]], back_all[pair_target[:, 1]]
+    grad_tokens = (first[:, :part_width] + second[:, :part_width]).astype(jnp.bfloat16)
+    grad_route = jnp.stack([first[:, part_width], second[:, part_width]], axis=1)
     return (grad_tokens, grad_route, grad_gate, grad_up, grad_down)
 
 

time: 352 us -> 350 us (level)
    another operation x3 -> x2, local copies, waits for them, and re-layouts: 11.6 us -> 11.5 us
  transfers between devices with their start and end apart: 4 -> 4, of which waited for: 1 -> 1; matrix products, arithmetic and copies ran while one was open for 27% -> 26% of each run, Pallas kernels for 32% -> 33%
where the time goes in v2:
time: 350 us; the launch traced here: 348 us
  Pallas kernels  114 us (33%)
  blocking collectives  61.3 us (18%)
  local copies, waits for them, and re-layouts  55.2 us (16%)
  matrix products  40.7 us (12%)
  other arithmetic  35.2 us (10%)
  waiting for transfers between devices  16.3 us (5%)
  between operations  14.5 us (4%)
  starting transfers between devices  11.2 us (3%)
    pallas_call x1, Pallas kernels, exchange_rows(): pl.pallas_call(functools.partial(exchange_kernel, n_seq, n_tx, peers), ou...  114 us
    all_to_all x1, blocking collectives, shards(): ring = lax.all_to_all(pair, 'tx', split_axis=0, concat_axis=0, tiled=True)  50.1 us
    all_to_all x1, waiting for transfers between devices, shards(): lax.all_to_all(back_send, ('expert', 'seq'), split_axis=0, concat_axis=0,...  16.2 us
    another operation x2, local copies, waits for them, and re-layouts  11.5 us
    all_to_all x1, blocking collectives, shards(): lax.all_to_all(stacked, 'core', split_axis=1, concat_axis=1, tiled=True)  11.3 us
    convert_element_type x1, local copies, waits for them, and re-layouts, shards(): scaled = (prob[None] * out_rows.astype(jnp.float32)).astype(jnp.bfloat16)  11.2 us
    dot_general x1, matrix products, shards(): jnp.einsum('emf,ecdf->ecdm', gate_grad, gate_p, preferred_element_type=jn...  9.57 us
    dot_general x1, matrix products, shards(): jnp.einsum('emf,ecdf->ecdm', up_grad, up_p, preferred_element_type=jnp.fl...  9.16 us
  transfers between devices with their start and end apart: 4, of which 1 were waited for; matrix products, arithmetic and copies ran while one was open for 26% of the time, Pallas kernels for 33%

profile of v2, /device:TPU:0, one launch (start us, length us, event | category | flops | bytes accessed | tf_op | source)
XLA Modules:
  0.0 348.4 jit_solution(13712452518991694684)
XLA Ops:
  7.2 3.5 %pad_maximum_fusion.1 = bf16[3,1,1792,256]{3,2,1,0:T(8,128)(2,1)} fusion(bf16[1,1,1792,256]{3,2,1,0:T(8,128)(2,1)} %bitcast.119, bf16[1,1,1792,256]{3,2,1,0:T(8,128)(2,1)} %bitcast.120, bf16[1,1,1792,256]{3,2,1,0:T(8,128)(2,1)} %bitcast.121), kind=kLoop, calls=%fused_computation.20 | loop fusion | flops 2752512 | bytes 5505024 | tf_op jit(solution)/shard_map/stack | solution.py:215
  13.7 2.9 scatter_custom_fusion
  16.7 3.5 %gather_fusion = bf16[512]{0:T(512)(128)(2,1)S(1)} fusion(bf16[384]{0:T(512)(128)(2,1)S(1)} %reshape.378, s32[1024]{0:T(1024)S(1)} %get-tuple-element.64), kind=kCustom, calls=%fused_computation | custom fusion | bytes 4096 | tf_op jit(solution)/shard_map/gather | solution.py:183
  21.5 2.7 gather_fusion.2
  24.2 2.7 gather_fusion.1
  26.9 114.1 %shard_map.110 = (bf16[8,16,32,896]{3,2,1,0:T(8,128)(2,1)}, bf16[8,16,32,896]{3,2,1,0:T(8,128)(2,1)}) custom-call(bf16[16,32,896]{2,1,0:T(8,128)(2,1)} %bitcast.115, bf16[16,32,896]{2,1,0:T(8,128)(2,1)} %bitcast.114), custom_call_target="tpu_custom_call" | custom-call | tf_op jit(solution)/shard_map/pallas_call | solution.py:137
  141.6 4.2 %all-to-all-start = ((bf16[16,1,32]{2,1,0:T(2,128)(2,1)}), bf16[16,1,32]{2,1,0:T(2,128)(2,1)S(1)}, u32[]{:S(2)}, u32[]{:S(2)}) async-start(bf16[16,1,32]{2,1,0:T(2,128)(2,1)} %copy.89), calls=%async_computation | async-start | bytes 16384 | tf_op jit(solution)/shard_map/all_to_all | solution.py:208
  145.8 11.3 %copy.88 = bf16[8,512,896]{1,2,0:T(8,128)(2,1)} copy(bf16[8,512,896]{2,1,0:T(8,128)(2,1)} %bitcast.107) | data formatting | bytes 14680064 | tf_op jit(solution)/shard_map/reshape.60
  157.2 8.4 %multiply_convert_fusion = bf16[8,16,32,896]{3,2,1,0:T(8,128)(2,1)} fusion(bf16[8,16,32,896]{3,2,1,0:T(8,128)(2,1)} %get-tuple-element.27, f32[16,32]{1,0:T(8,128)S(1)} %bitcast.122), kind=kLoop, calls=%fused_computation.6 | loop fusion | flops 11010048 | bytes 14682112 | tf_op jit(solution)/shard_map/convert_element_type | solution.py:231
  165.6 11.2 %copy.93 = bf16[8,512,896]{1,2,0:T(8,128)(2,1)} copy(bf16[8,512,896]{2,1,0:T(8,128)(2,1)} %bitcast.99) | data formatting | bytes 14680064 | tf_op jit(solution)/shard_map/convert_element_type | solution.py:231
  176.8 4.8 %fusion.35 = (bf16[1,1,7168,256]{3,2,1,0:T(8,128)(2,1)S(1)}, bf16[1,1,7168,256]{3,2,1,0:T(8,128)(2,1)S(1)}, bf16[1,1,7168,256]{3,2,1,0:T(8,128)(2,1)S(1)}) fusion(bf16[3,1,7168,256]{3,2,1,0:T(8,128)(2,1)} %all-gather.2.cloned.1.call-done), kind=kLoop, calls=%fused_computation.93 | loop fusion | bytes 22020096 | tf_op jit(solution)/shard_map/slice | solution.py:217
  181.6 7.9 %convolution_bitcast_fusion = f32[512,256]{0,1:T(8,128)S(1)} fusion(bf16[8,512,896]{2,1,0:T(8,128)(2,1)} %bitcast.108, bf16[8,896,256]{2,1,0:T(8,128)(2,1)S(1)} %bitcast.102), kind=kOutput, calls=%fused_computation.24 | convolution fusion | flops 1879048192 | bytes 11534336 | tf_op jit(solution)/shard_map/cemd,ecdf->emf/dot_general | solution.py:223
  189.5 5.4 %convolution_bitcast_fusion.1 = f32[512,256]{0,1:T(8,128)S(1)} fusion(bf16[8,512,896]{2,1,0:T(8,128)(2,1)} %bitcast.109, bf16[8,896,256]{2,1,0:T(8,128)(2,1)S(1)} %bitcast.100), kind=kOutput, calls=%fused_computation.25 | convolution fusion | flops 1879048192 | bytes 11534336 | tf_op jit(solution)/shard_map/cemd,ecdf->emf/dot_general | solution.py:224
  195.0 2.3 multiply_reduce_fusion
  197.3 2.1 fusion.1
  199.5 2.1 fusion
  201.6 2.2 fusion.2
  203.8 5.2 %pad_maximum_fusion = bf16[3,1,7168,256]{3,2,1,0:T(8,128)(2,1)} fusion(bf16[1,1,7168,256]{3,2,1,0:T(8,128)(2,1)S(1)} %fusion.2, bf16[1,1,7168,256]{3,2,1,0:T(8,128)(2,1)S(1)} %fusion.1, bf16[1,1,7168,256]{3,2,1,0:T(8,128)(2,1)S(1)} %fusion), kind=kLoop, calls=%fused_computation.7 | loop fusion | flops 11010048 | bytes 22020096 | tf_op jit(solution)/shard_map/stack | solution.py:240
  209.0 9.6 %fusion.4 = f32[8,912,512]{2,1,0:T(8,128)} fusion(bf16[1,8,896,256]{3,2,1,0:T(8,128)(2,1)} %bitcast.103, bf16[1,512,256]{1,2,0:T(8,128)(2,1)S(1)} %bitcast.118), kind=kOutput, calls=%fused_computation.16 | convolution fusion | flops 1912602624 | bytes 18874368 | tf_op jit(solution)/shard_map/emf,ecdf->ecdm/dot_general | solution.py:250
  218.6 9.2 %convolution_add_fusion = bf16[8,912,512]{2,1,0:T(8,128)(2,1)} fusion(f32[8,912,512]{2,1,0:T(8,128)} %fusion.4, bf16[1,8,896,256]{3,2,1,0:T(8,128)(2,1)S(1)} %bitcast.101, bf16[1,512,256]{1,2,0:T(8,128)(2,1)S(1)} %bitcast.117), kind=kOutput, calls=%fused_computation.11 | convolution fusion | flops 1920073728 | bytes 26345472 | tf_op jit(solution)/shard_map/emf,ecdf->ecdm/dot_general | solution.py:253
  227.7 1.5 scatter.13
  229.3 3.7 %copy.96 = bf16[4,2,912,512]{3,2,0,1:T(8,128)(2,1)S(1)} copy(bf16[4,2,912,512]{3,2,1,0:T(8,128)(2,1)} %bitcast.98) | data formatting | bytes 14942208 | tf_op jit(solution)/shard_map/reshape | solution.py:262
  233.0 11.3 %all_to_all.24 = bf16[4,2,912,512]{3,2,0,1:T(8,128)(2,1)} all-to-all(bf16[4,2,912,512]{3,2,0,1:T(8,128)(2,1)S(1)} %copy.96), channel_id=1, replica_groups=mesh['expert'=4,'seq'=4,'tx'=4,'core'=2] {'core'}, dimensions={1} | all-to-all | bytes 14942208 | tf_op jit(solution)/shard_map/all_to_all | solution.py:263
  244.3 7.9 %reduce_sum.49 = bf16[4,912,512]{2,1,0:T(8,128)(2,1)} reduce(bf16[4,2,912,512]{3,2,0,1:T(8,128)(2,1)} %all_to_all.24, bf16[]{:T(256)} %constant.116.clone.1), dimensions={1}, to_apply=%region_5.6 | reduce | flops 1867776 | bytes 11206658 | tf_op jit(solution)/shard_map/reduce_sum | solution.py:264
  252.2 50.1 %all_to_all.25 = bf16[4,912,512]{2,1,0:T(8,128)(2,1)} all-to-all(bf16[4,912,512]{2,1,0:T(8,128)(2,1)} %reduce_sum.49), channel_id=1, replica_groups=mesh['expert'=4,'seq'=4,'tx'=4,'core'=2] {'tx'}, dimensions={0} | all-to-all | bytes 7471104 | tf_op jit(solution)/shard_map/all_to_all | solution.py:265
  302.2 3.2 reduce_sum.50
  306.7 6.9 %all-to-all-start.3 = ((bf16[16,32,912]{2,1,0:T(8,128)(2,1)}), bf16[16,32,912]{2,1,0:T(8,128)(2,1)S(1)}, u32[]{:S(2)}, u32[]{:S(2)}) async-start(bf16[16,32,912]{2,1,0:T(8,128)(2,1)} %bitcast.37), calls=%async_computation.3 | async-start | bytes 2097152 | tf_op jit(solution)/shard_map/all_to_all | solution.py:270
  313.9 16.2 %all-to-all-done.3 = bf16[16,32,912]{2,1,0:T(8,128)(2,1)S(1)} async-done(((bf16[16,32,912]{2,1,0:T(8,128)(2,1)}), bf16[16,32,912]{2,1,0:T(8,128)(2,1)S(1)}, u32[]{:S(2)}, u32[]{:S(2)}) %all-to-all-start.3) | async-done | bytes 933920 | tf_op jit(solution)/shard_map/all_to_all | solution.py:270
  331.4 1.8 gather_fusion.3
  334.8 1.9 fusion.8
  336.7 2.2 convert_element_type.103
  339.0 2.6 slice_bitcast_fusion
  (68 shorter events, 9.4 us)
Async XLA Ops:
  7.2 169.6 %all-gather.2.cloned.1.call-start = ((), (), s32[]{:S(2)}) async-start(), calls=%async_computation.5 | async-start | bytes 13762560 | tf_op jit(solution)/shard_map/all_gather | solution.py:214
  7.2 3.6 %copy-start.3 = (s32[192,2]{0,1:T(2,128)S(1)}, s32[192,2]{0,1:T(2,128)}, u32[]{:S(2)}) copy-start(s32[192,2]{0,1:T(2,128)} %param.11) | copy-start | bytes 4612
  7.2 4.0 %copy-start.4 = (bf16[192,2]{0,1:T(2,128)(2,1)S(1)}, bf16[192,2]{0,1:T(2,128)(2,1)}, u32[]{:S(2)}) copy-start(bf16[192,2]{0,1:T(2,128)(2,1)} %param.12) | copy-start | bytes 2308
  141.6 15.5 %all-to-all-start = ((bf16[16,1,32]{2,1,0:T(2,128)(2,1)}), bf16[16,1,32]{2,1,0:T(2,128)(2,1)S(1)}, u32[]{:S(2)}, u32[]{:S(2)}) async-start(bf16[16,1,32]{2,1,0:T(2,128)(2,1)} %copy.89), calls=%async_computation | async-start | bytes 16384 | tf_op jit(solution)/shard_map/all_to_all | solution.py:208
  145.8 191.0 %reduce-scatter.2.cloned.1.call-start = ((), (), s32[]{:S(2)}) async-start(), calls=%async_computation.6 | async-start | bytes 13762560 | tf_op jit(solution)/shard_map/reduce_scatter | solution.py:244
  181.6 7.9 %copy-start.2 = (bf16[1,1,7168,256]{3,2,1,0:T(8,128)(2,1)}, bf16[1,1,7168,256]{3,2,1,0:T(8,128)(2,1)S(1)}, u32[]{:S(2)}) copy-start(bf16[1,1,7168,256]{3,2,1,0:T(8,128)(2,1)S(1)} %get-tuple-element.50) | copy-start | bytes 11010052
  181.6 7.9 %copy-start = (bf16[1,1,7168,256]{3,2,1,0:T(8,128)(2,1)}, bf16[1,1,7168,256]{3,2,1,0:T(8,128)(2,1)S(1)}, u32[]{:S(2)}) copy-start(bf16[1,1,7168,256]{3,2,1,0:T(8,128)(2,1)S(1)} %get-tuple-element.49) | copy-start | bytes 11010052
  181.6 13.4 %slice-start.2 = ((s8[7340032]{0:T(1024)(128)(4,1)}), s8[4194304]{0:T(1024)(128)(4,1)S(1)}, s32[]{:S(2)}) async-start(s8[7340032]{0:T(1024)(128)(4,1)} %bitcast.104), calls=%async_computation.9 | async-start | bytes 8388608
  189.5 5.4 %slice-start.3 = ((s8[7340032]{0:T(1024)(128)(4,1)}), s8[3145728]{0:T(1024)(128)(4,1)S(1)}, s32[]{:S(2)}) async-start(s8[7340032]{0:T(1024)(128)(4,1)} %bitcast.104), calls=%async_computation.10 | async-start | bytes 6291456
  189.5 7.8 %slice-start = ((s8[7340032]{0:T(1024)(128)(4,1)}), s8[4194304]{0:T(1024)(128)(4,1)S(1)}, s32[]{:S(2)}) async-start(s8[7340032]{0:T(1024)(128)(4,1)} %bitcast.94), calls=%async_computation.7 | async-start | bytes 8388608
  195.0 2.3 slice-start.1
  197.3 4.2 %slice-start.4 = ((s8[7340032]{0:T(1024)(128)(4,1)}), s8[4194304]{0:T(1024)(128)(4,1)S(1)}, s32[]{:S(2)}) async-start(s8[7340032]{0:T(1024)(128)(4,1)} %bitcast.110), calls=%async_computation.11 | async-start | bytes 8388608
  199.4 2.1 slice-start.5
  209.0 9.6 %copy-start.1 = (bf16[1,1,7168,256]{3,2,1,0:T(8,128)(2,1)S(1)}, bf16[1,1,7168,256]{3,2,1,0:T(8,128)(2,1)}, u32[]{:S(2)}) copy-start(bf16[1,1,7168,256]{3,2,1,0:T(8,128)(2,1)} %copy-done) | copy-start | bytes 11010052
  306.7 23.4 %all-to-all-start.3 = ((bf16[16,32,912]{2,1,0:T(8,128)(2,1)}), bf16[16,32,912]{2,1,0:T(8,128)(2,1)S(1)}, u32[]{:S(2)}, u32[]{:S(2)}) async-start(bf16[16,32,912]{2,1,0:T(8,128)(2,1)} %bitcast.37), calls=%async_computation.3 | async-start | bytes 2097152 | tf_op jit(solution)/shard_map/all_to_all | solution.py:270
Sparse Core Ops, SparseCore 0:
  10.9 127.4 all-gather.1
  209.1 103.2 reduce-scatter.1

commit v3 on v2

--- a/solution.py
+++ b/solution.py
@@ -241,8 +241,8 @@
         3, local_count, model_width, hidden_count
     ).astype(jnp.bfloat16)
     parts, gate_grad, up_grad = lax.optimization_barrier((parts, gate_grad, up_grad))
-    reduced_parts = lax.psum_scatter(parts, "seq", scatter_dimension=2, tiled=True).astype(jnp.float32)
-    grad_gate, grad_up, grad_down = reduced_parts[0], reduced_parts[1], reduced_parts[2]
+    reduced_parts = lax.psum_scatter(parts, "seq", scatter_dimension=2, tiled=True)
+    grad_gate, grad_up, grad_down = (reduced_parts[w].astype(jnp.float32) for w in range(3))
     score_pad = 16
     gate_p, up_p = (
         jnp.pad(w, ((0, 0), (0, 0), (0, score_pad), (0, 0))) for w in (gate_h, up_h)

time: 350 us -> 349 us (level)
  no operation moved by 1% of the time
where the time goes in v3:
time: 349 us; the launch traced here: 348 us
  Pallas kernels  114 us (33%)
  blocking collectives  61.3 us (18%)
  local copies, waits for them, and re-layouts  52.6 us (15%)
  matrix products  40.7 us (12%)
  other arithmetic  37.2 us (11%)
  waiting for transfers between devices  16.3 us (5%)
  between operations  14.5 us (4%)
  starting transfers between devices  11.2 us (3%)
    pallas_call x1, Pallas kernels, exchange_rows(): pl.pallas_call(functools.partial(exchange_kernel, n_seq, n_tx, peers), ou...  114 us
    all_to_all x1, blocking collectives, shards(): ring = lax.all_to_all(pair, 'tx', split_axis=0, concat_axis=0, tiled=True)  50.1 us
    all_to_all x1, waiting for transfers between devices, shards(): lax.all_to_all(back_send, ('expert', 'seq'), split_axis=0, concat_axis=0,...  16.2 us
    another operation x2, local copies, waits for them, and re-layouts  11.5 us
    all_to_all x1, blocking collectives, shards(): lax.all_to_all(stacked, 'core', split_axis=1, concat_axis=1, tiled=True)  11.3 us
    convert_element_type x1, local copies, waits for them, and re-layouts, shards(): scaled = (prob[None] * out_rows.astype(jnp.float32)).astype(jnp.bfloat16)  11.2 us
    dot_general x1, matrix products, shards(): jnp.einsum('emf,ecdf->ecdm', gate_grad, gate_p, preferred_element_type=jn...  9.57 us
    dot_general x1, matrix products, shards(): jnp.einsum('emf,ecdf->ecdm', up_grad, up_p, preferred_element_type=jnp.fl...  9.16 us
  transfers between devices with their start and end apart: 4, of which 1 were waited for; matrix products, arithmetic and copies ran while one was open for 26% of the time, Pallas kernels for 33%

profile of v3, /device:TPU:0, one launch (start us, length us, event | category | flops | bytes accessed | tf_op | source)
XLA Modules:
  0.0 347.9 jit_solution(3636239876585272207)
XLA Ops:
  7.2 3.5 %pad_maximum_fusion.1 = bf16[3,1,1792,256]{3,2,1,0:T(8,128)(2,1)} fusion(bf16[1,1,1792,256]{3,2,1,0:T(8,128)(2,1)} %bitcast.128, bf16[1,1,1792,256]{3,2,1,0:T(8,128)(2,1)} %bitcast.129, bf16[1,1,1792,256]{3,2,1,0:T(8,128)(2,1)} %bitcast.130), kind=kLoop, calls=%fused_computation.20 | loop fusion | flops 2752512 | bytes 5505024 | tf_op jit(solution)/shard_map/stack | solution.py:215
  13.7 2.9 scatter_custom_fusion
  16.7 3.5 %gather_fusion = bf16[512]{0:T(512)(128)(2,1)S(1)} fusion(bf16[384]{0:T(512)(128)(2,1)S(1)} %reshape.420, s32[1024]{0:T(1024)S(1)} %get-tuple-element.64), kind=kCustom, calls=%fused_computation | custom fusion | bytes 4096 | tf_op jit(solution)/shard_map/gather | solution.py:183
  21.5 2.7 gather_fusion.2
  24.2 2.7 gather_fusion.1
  26.9 114.1 %shard_map.110 = (bf16[8,16,32,896]{3,2,1,0:T(8,128)(2,1)}, bf16[8,16,32,896]{3,2,1,0:T(8,128)(2,1)}) custom-call(bf16[16,32,896]{2,1,0:T(8,128)(2,1)} %bitcast.124, bf16[16,32,896]{2,1,0:T(8,128)(2,1)} %bitcast.123), custom_call_target="tpu_custom_call" | custom-call | tf_op jit(solution)/shard_map/pallas_call | solution.py:137
  141.6 4.2 %all-to-all-start = ((bf16[16,1,32]{2,1,0:T(2,128)(2,1)}), bf16[16,1,32]{2,1,0:T(2,128)(2,1)S(1)}, u32[]{:S(2)}, u32[]{:S(2)}) async-start(bf16[16,1,32]{2,1,0:T(2,128)(2,1)} %copy.89), calls=%async_computation | async-start | bytes 16384 | tf_op jit(solution)/shard_map/all_to_all | solution.py:208
  145.8 11.3 %copy.88 = bf16[8,512,896]{1,2,0:T(8,128)(2,1)} copy(bf16[8,512,896]{2,1,0:T(8,128)(2,1)} %bitcast.116) | data formatting | bytes 14680064 | tf_op jit(solution)/shard_map/reshape.60
  157.2 8.4 %multiply_convert_fusion = bf16[8,16,32,896]{3,2,1,0:T(8,128)(2,1)} fusion(bf16[8,16,32,896]{3,2,1,0:T(8,128)(2,1)} %get-tuple-element.27, f32[16,32]{1,0:T(8,128)S(1)} %bitcast.131), kind=kLoop, calls=%fused_computation.6 | loop fusion | flops 11010048 | bytes 14682112 | tf_op jit(solution)/shard_map/convert_element_type | solution.py:231
  165.6 11.2 %copy.93 = bf16[8,512,896]{1,2,0:T(8,128)(2,1)} copy(bf16[8,512,896]{2,1,0:T(8,128)(2,1)} %bitcast.108) | data formatting | bytes 14680064 | tf_op jit(solution)/shard_map/convert_element_type | solution.py:231
  176.8 4.8 %fusion.38 = (bf16[1,1,7168,256]{3,2,1,0:T(8,128)(2,1)S(1)}, bf16[1,1,7168,256]{3,2,1,0:T(8,128)(2,1)S(1)}, bf16[1,1,7168,256]{3,2,1,0:T(8,128)(2,1)S(1)}) fusion(bf16[3,1,7168,256]{3,2,1,0:T(8,128)(2,1)} %all-gather.2.cloned.1.call-done), kind=kLoop, calls=%fused_computation.96 | loop fusion | bytes 22020096 | tf_op jit(solution)/shard_map/slice | solution.py:217
  181.6 7.9 %convolution_bitcast_fusion = f32[512,256]{0,1:T(8,128)S(1)} fusion(bf16[8,512,896]{2,1,0:T(8,128)(2,1)} %bitcast.117, bf16[8,896,256]{2,1,0:T(8,128)(2,1)S(1)} %bitcast.111), kind=kOutput, calls=%fused_computation.21 | convolution fusion | flops 1879048192 | bytes 11534336 | tf_op jit(solution)/shard_map/cemd,ecdf->emf/dot_general | solution.py:223
  189.5 5.4 %convolution_bitcast_fusion.1 = f32[512,256]{0,1:T(8,128)S(1)} fusion(bf16[8,512,896]{2,1,0:T(8,128)(2,1)} %bitcast.118, bf16[8,896,256]{2,1,0:T(8,128)(2,1)S(1)} %bitcast.109), kind=kOutput, calls=%fused_computation.22 | convolution fusion | flops 1879048192 | bytes 11534336 | tf_op jit(solution)/shard_map/cemd,ecdf->emf/dot_general | solution.py:224
  195.0 2.3 multiply_reduce_fusion
  197.3 2.1 fusion.1
  199.5 2.1 fusion
  201.6 2.2 fusion.2
  203.8 5.2 %pad_maximum_fusion = bf16[3,1,7168,256]{3,2,1,0:T(8,128)(2,1)} fusion(bf16[1,1,7168,256]{3,2,1,0:T(8,128)(2,1)S(1)} %fusion.2, bf16[1,1,7168,256]{3,2,1,0:T(8,128)(2,1)S(1)} %fusion.1, bf16[1,1,7168,256]{3,2,1,0:T(8,128)(2,1)S(1)} %fusion), kind=kLoop, calls=%fused_computation.7 | loop fusion | flops 11010048 | bytes 22020096 | tf_op jit(solution)/shard_map/stack | solution.py:240
  209.0 9.6 %fusion.4 = f32[8,912,512]{2,1,0:T(8,128)} fusion(bf16[1,8,896,256]{3,2,1,0:T(8,128)(2,1)} %bitcast.112, bf16[1,512,256]{1,2,0:T(8,128)(2,1)S(1)} %bitcast.127), kind=kOutput, calls=%fused_computation.16 | convolution fusion | flops 1912602624 | bytes 18874368 | tf_op jit(solution)/shard_map/emf,ecdf->ecdm/dot_general | solution.py:250
  218.6 9.2 %convolution_add_fusion = bf16[8,912,512]{2,1,0:T(8,128)(2,1)} fusion(f32[8,912,512]{2,1,0:T(8,128)} %fusion.4, bf16[1,8,896,256]{3,2,1,0:T(8,128)(2,1)S(1)} %bitcast.110, bf16[1,512,256]{1,2,0:T(8,128)(2,1)S(1)} %bitcast.126), kind=kOutput, calls=%fused_computation.11 | convolution fusion | flops 1920073728 | bytes 26345472 | tf_op jit(solution)/shard_map/emf,ecdf->ecdm/dot_general | solution.py:253
  227.7 1.5 scatter.13
  229.3 3.7 %copy.96 = bf16[4,2,912,512]{3,2,0,1:T(8,128)(2,1)S(1)} copy(bf16[4,2,912,512]{3,2,1,0:T(8,128)(2,1)} %bitcast.107) | data formatting | bytes 14942208 | tf_op jit(solution)/shard_map/reshape | solution.py:262
  233.0 11.3 %all_to_all.24 = bf16[4,2,912,512]{3,2,0,1:T(8,128)(2,1)} all-to-all(bf16[4,2,912,512]{3,2,0,1:T(8,128)(2,1)S(1)} %copy.96), channel_id=1, replica_groups=mesh['expert'=4,'seq'=4,'tx'=4,'core'=2] {'core'}, dimensions={1} | all-to-all | bytes 14942208 | tf_op jit(solution)/shard_map/all_to_all | solution.py:263
  244.3 7.9 %reduce_sum.49 = bf16[4,912,512]{2,1,0:T(8,128)(2,1)} reduce(bf16[4,2,912,512]{3,2,0,1:T(8,128)(2,1)} %all_to_all.24, bf16[]{:T(256)} %constant.116.clone.1), dimensions={1}, to_apply=%region_5.6 | reduce | flops 1867776 | bytes 11206658 | tf_op jit(solution)/shard_map/reduce_sum | solution.py:264
  252.2 50.1 %all_to_all.25 = bf16[4,912,512]{2,1,0:T(8,128)(2,1)} all-to-all(bf16[4,912,512]{2,1,0:T(8,128)(2,1)} %reduce_sum.49), channel_id=1, replica_groups=mesh['expert'=4,'seq'=4,'tx'=4,'core'=2] {'tx'}, dimensions={0} | all-to-all | bytes 7471104 | tf_op jit(solution)/shard_map/all_to_all | solution.py:265
  302.2 3.2 reduce_sum.50
  305.4 1.3 copy.97
  306.7 6.9 %all-to-all-start.3 = ((bf16[16,32,912]{2,1,0:T(8,128)(2,1)}), bf16[16,32,912]{2,1,0:T(8,128)(2,1)S(1)}, u32[]{:S(2)}, u32[]{:S(2)}) async-start(bf16[16,32,912]{2,1,0:T(8,128)(2,1)} %bitcast.37), calls=%async_computation.3 | async-start | bytes 2097152 | tf_op jit(solution)/shard_map/all_to_all | solution.py:270
  313.9 16.2 %all-to-all-done.3 = bf16[16,32,912]{2,1,0:T(8,128)(2,1)S(1)} async-done(((bf16[16,32,912]{2,1,0:T(8,128)(2,1)}), bf16[16,32,912]{2,1,0:T(8,128)(2,1)S(1)}, u32[]{:S(2)}, u32[]{:S(2)}) %all-to-all-start.3) | async-done | bytes 933920 | tf_op jit(solution)/shard_map/all_to_all | solution.py:270
  331.4 1.8 gather_fusion.3
  334.8 1.9 fusion.11
  336.7 4.3 %fusion.8 = (f32[1,1792,256]{2,1,0:T(8,128)}, f32[1,1792,256]{2,1,0:T(8,128)}, f32[1,1792,256]{2,1,0:T(8,128)}) fusion(bf16[3,1,1792,256]{3,2,1,0:T(8,128)(2,1)} %reduce-scatter.2.cloned.1.call-done), kind=kLoop, calls=%fused_computation.26 | loop fusion | flops 1376256 | bytes 8257536 | tf_op jit(solution)/shard_map/convert_element_type | solution.py:245
  (67 shorter events, 8.1 us)
Async XLA Ops:
  7.2 169.6 %all-gather.2.cloned.1.call-start = ((), (), s32[]{:S(2)}) async-start(), calls=%async_computation.5 | async-start | bytes 13762560 | tf_op jit(solution)/shard_map/all_gather | solution.py:214
  7.2 3.6 %copy-start.3 = (s32[192,2]{0,1:T(2,128)S(1)}, s32[192,2]{0,1:T(2,128)}, u32[]{:S(2)}) copy-start(s32[192,2]{0,1:T(2,128)} %param.11) | copy-start | bytes 4612
  7.2 4.0 %copy-start.4 = (bf16[192,2]{0,1:T(2,128)(2,1)S(1)}, bf16[192,2]{0,1:T(2,128)(2,1)}, u32[]{:S(2)}) copy-start(bf16[192,2]{0,1:T(2,128)(2,1)} %param.12) | copy-start | bytes 2308
  141.6 15.5 %all-to-all-start = ((bf16[16,1,32]{2,1,0:T(2,128)(2,1)}), bf16[16,1,32]{2,1,0:T(2,128)(2,1)S(1)}, u32[]{:S(2)}, u32[]{:S(2)}) async-start(bf16[16,1,32]{2,1,0:T(2,128)(2,1)} %copy.89), calls=%async_computation | async-start | bytes 16384 | tf_op jit(solution)/shard_map/all_to_all | solution.py:208
  145.8 191.0 %reduce-scatter.2.cloned.1.call-start = ((), (), s32[]{:S(2)}) async-start(), calls=%async_computation.6 | async-start | bytes 13762560 | tf_op jit(solution)/shard_map/reduce_scatter | solution.py:244
  181.6 7.9 %copy-start.2 = (bf16[1,1,7168,256]{3,2,1,0:T(8,128)(2,1)}, bf16[1,1,7168,256]{3,2,1,0:T(8,128)(2,1)S(1)}, u32[]{:S(2)}) copy-start(bf16[1,1,7168,256]{3,2,1,0:T(8,128)(2,1)S(1)} %get-tuple-element.50) | copy-start | bytes 11010052
  181.6 7.9 %copy-start = (bf16[1,1,7168,256]{3,2,1,0:T(8,128)(2,1)}, bf16[1,1,7168,256]{3,2,1,0:T(8,128)(2,1)S(1)}, u32[]{:S(2)}) copy-start(bf16[1,1,7168,256]{3,2,1,0:T(8,128)(2,1)S(1)} %get-tuple-element.49) | copy-start | bytes 11010052
  181.6 13.4 %slice-start.2 = ((s8[7340032]{0:T(1024)(128)(4,1)}), s8[4194304]{0:T(1024)(128)(4,1)S(1)}, s32[]{:S(2)}) async-start(s8[7340032]{0:T(1024)(128)(4,1)} %bitcast.113), calls=%async_computation.9 | async-start | bytes 8388608
  189.5 5.4 %slice-start.3 = ((s8[7340032]{0:T(1024)(128)(4,1)}), s8[3145728]{0:T(1024)(128)(4,1)S(1)}, s32[]{:S(2)}) async-start(s8[7340032]{0:T(1024)(128)(4,1)} %bitcast.113), calls=%async_computation.10 | async-start | bytes 6291456
  189.5 7.8 %slice-start = ((s8[7340032]{0:T(1024)(128)(4,1)}), s8[4194304]{0:T(1024)(128)(4,1)S(1)}, s32[]{:S(2)}) async-start(s8[7340032]{0:T(1024)(128)(4,1)} %bitcast.103), calls=%async_computation.7 | async-start | bytes 8388608
  195.0 2.3 slice-start.1
  197.3 4.2 %slice-start.4 = ((s8[7340032]{0:T(1024)(128)(4,1)}), s8[4194304]{0:T(1024)(128)(4,1)S(1)}, s32[]{:S(2)}) async-start(s8[7340032]{0:T(1024)(128)(4,1)} %bitcast.119), calls=%async_computation.11 | async-start | bytes 8388608
  199.4 2.1 slice-start.5
  209.0 9.6 %copy-start.1 = (bf16[1,1,7168,256]{3,2,1,0:T(8,128)(2,1)S(1)}, bf16[1,1,7168,256]{3,2,1,0:T(8,128)(2,1)}, u32[]{:S(2)}) copy-start(bf16[1,1,7168,256]{3,2,1,0:T(8,128)(2,1)} %copy-done) | copy-start | bytes 11010052
  306.7 23.4 %all-to-all-start.3 = ((bf16[16,32,912]{2,1,0:T(8,128)(2,1)}), bf16[16,32,912]{2,1,0:T(8,128)(2,1)S(1)}, u32[]{:S(2)}, u32[]{:S(2)}) async-start(bf16[16,32,912]{2,1,0:T(8,128)(2,1)} %bitcast.37), calls=%async_computation.3 | async-start | bytes 2097152 | tf_op jit(solution)/shard_map/all_to_all | solution.py:270
Sparse Core Ops, SparseCore 0:
  10.9 127.4 all-gather.1
  209.1 103.2 reduce-scatter.1
